TPU v7x, 256 devices: a whole 4x4x8 slice. The times are simulated.
256 devices in a mesh: pb: 64 (over z, y_hi, x), br: 4 (over y_lo, core).
Axes of the slice: x: 4, y: 4 (y_hi: 2, y_lo: 2; y = y_hi * 2 + y_lo), z: 8, core: 2. Of those that a mesh axis runs over, the one named last changes fastest.
Arguments:
- bloch_const: bfloat16 [36, 663552], P(None, 'pb'), may hold values from -1 to 1
- polarization: bfloat16 [36, 512, 36], P('br', 'pb'), may hold values from -1 to 1
- delta_weight: bfloat16 [36, 512, 18432], P('br', None, 'pb'), may hold values from 0.02 to 3
- partner: int32 [512, 512], P('pb'), may hold values from 0 to 511, each once within a row
- velocity: float32 [512, 36], P('pb', 'br'), may hold values from -0.5 to 1.5
- capacity: float32 [512, 36], P('pb', 'br'), may hold values from 0.2 to 2
Outputs:
- deviation: float32 [512, 36], P('pb', 'br')
- kappa: float32 [2], replicated
Inputs may be any that keep to these rules, and one draw needn't show every extreme that they name: For each q, partner[q, :] names every q-point exactly once.
All inputs are finite; a program needn't handle non-finite values.
Results may differ from a plain program's by a relative error of at most 0.0003.
Values may be sent and summed in bfloat16 or wider, within the bound.
A program may use at most 192 MiB of HBM per device.

v0:
```python
from functools import partial

import jax
import jax.numpy as jnp
from jax import lax
from jax.sharding import PartitionSpec as P

ITERS = 2


def split_points(bloch_const, local_points, chosen):
    components = bloch_const.shape[0]
    reshaped = bloch_const.reshape(components, local_points, -1, components)
    return jnp.transpose(reshaped.reshape(components, local_points, chosen * components), (1, 0, 2))


def coupling_fold(carried, shard_in, first_row, const_blocks, delta_local, inv_count):
    lead_size = shard_in.shape[0]
    piece_len = shard_in.shape[1]
    components = shard_in.shape[2]
    flat_rows = shard_in.reshape(lead_size * piece_len, components)

    def per_point(const_block):
        amplitude = jnp.dot(flat_rows, const_block, preferred_element_type=jnp.float32)
        amplitude = amplitude.reshape(lead_size * piece_len, -1, components)
        return jnp.sum(amplitude * amplitude, axis=2)

    squared = lax.map(per_point, const_blocks)
    squared = jnp.transpose(squared, (1, 0, 2)).reshape(lead_size, piece_len, -1)
    weight_block = delta_local.astype(jnp.float32)
    return squared * weight_block * inv_count


def branch_total(partial_sum):
    own_count = partial_sum.shape[1] // lax.axis_size("br")
    summed = lax.psum(partial_sum, "br")
    return lax.dynamic_slice_in_dim(summed, lax.axis_index("br") * own_count, own_count, 1)


def full_deviation(deviation):
    return lax.all_gather(deviation, "pb", axis=0, tiled=True)


def on_device(bloch_const, polarization, delta_weight, partner, velocity, capacity):
    local_points = velocity.shape[0]
    own_count = velocity.shape[1]
    all_branches = own_count * lax.axis_size("br")
    total_points = polarization.shape[1] * lax.axis_size("pb")
    inv_count = 1.0 / (total_points * all_branches)
    const_blocks = split_points(bloch_const, local_points, all_branches)
    zero_start = jnp.zeros((own_count, total_points, local_points * all_branches), jnp.float32)
    folder = partial(
        coupling_fold, const_blocks=const_blocks, delta_local=delta_weight, inv_count=inv_count
    )
    coupling = folder(
        zero_start, lax.all_gather(polarization, "pb", axis=1, tiled=True), jnp.int32(0)
    )
    coupling = coupling.reshape(own_count, total_points, local_points, all_branches)
    rate_total = branch_total(jnp.sum(coupling, axis=(0, 1)))
    deviation = velocity / rate_total
    heat_weight = capacity * velocity
    kappas = []
    for sweep_index in range(ITERS):
        deviation_all = full_deviation(deviation)
        partner_value = deviation_all[partner]
        combined = jnp.transpose(deviation_all)[:, :, None] + jnp.transpose(
            partner_value, (2, 1, 0)
        )
        spread = jnp.einsum("abqs,abq->qs", coupling, combined, precision=lax.Precision.HIGHEST)
        spread = branch_total(spread)
        deviation = (velocity + 0.5 * spread) / rate_total
        kappa_term = jnp.sum(heat_weight * deviation) * inv_count
        kappas.append(lax.psum(kappa_term, ("pb", "br")))
    kappa = jnp.stack(kappas)
    return (deviation, kappa)


def solution(mesh):
    in_specs = (
        P(None, "pb"),
        P("br", "pb", None),
        P("br", None, "pb"),
        P("pb", None),
        P("pb", "br"),
        P("pb", "br"),
    )
    out_specs = (P("pb", "br"), P())
    return jax.shard_map(
        on_device, mesh=mesh, in_specs=in_specs, out_specs=out_specs, check_vma=False
    )
```

profile of v0, /device:TPU:1, one launch (start us, length us, event | category | flops | bytes accessed | tf_op | source)
XLA Modules:
  0.0 1065.5 jit_solution(7599198885120095185)
XLA Ops:
  3.1 163.8 %all_gather.9 = bf16[9,512,36]{2,1,0:T(8,128)(2,1)S(1)} all-gather(bf16[9,8,36]{2,1,0:T(8,128)(2,1)} %param.9), channel_id=1, replica_groups=mesh['pb'=64,'br'=4] {'pb'}, dimensions={1}, use_global_device_ids=true | all-gather | bytes 336960 | tf_op jit(solution)/shard_map/all_gather | solution.py:56
  166.9 349.9 %while.10 = (s32[]{:T(128)}, f32[8,4608,36]{1,2,0:T(8,128)}, bf16[8,36,1296]{2,1,0:T(8,128)(2,1)S(1)}, bf16[4608,36]{1,0:T(8,128)(2,1)S(1)}, s32[]{:T(128)}, /*index=5*/f32[]{:T(128)}) while((s32[]{:T(128)}, f32[8,4608,36]{1,2,0:T(8,128)}, bf16[8,36,1296]{2,1,0:T(8,128)(2,1)S(1)}, bf16[4608,36]{1,0:T(8,128)(2,1)S(1)}, s32[]{:T(128)}, ...), condition=%wide.region_2.3_spmd, body=%wide.region_0.2_spmd.sunk | while | flops 441759744 | bytes 98908744 | solution.py:28
  176.6 23.2 %mul.74 = f32[4608,36,36]{0,2,1:T(8,128)} reshape(f32[4608,1296]{0,1:T(8,128)} %fusion.18) | data formatting | bytes 47775744 | tf_op jit(solution)/shard_map/while/body/eval_jaxpr/mul | solution.py:26
  199.8 9.9 reduce_sum.46
  220.3 23.2 %mul.74 = f32[4608,36,36]{0,2,1:T(8,128)} reshape(f32[4608,1296]{0,1:T(8,128)} %fusion.18) | data formatting | bytes 47775744 | tf_op jit(solution)/shard_map/while/body/eval_jaxpr/mul | solution.py:26
  243.5 9.9 reduce_sum.46
  264.1 23.2 %mul.74 = f32[4608,36,36]{0,2,1:T(8,128)} reshape(f32[4608,1296]{0,1:T(8,128)} %fusion.18) | data formatting | bytes 47775744 | tf_op jit(solution)/shard_map/while/body/eval_jaxpr/mul | solution.py:26
  307.9 23.2 %mul.74 = f32[4608,36,36]{0,2,1:T(8,128)} reshape(f32[4608,1296]{0,1:T(8,128)} %fusion.18) | data formatting | bytes 47775744 | tf_op jit(solution)/shard_map/while/body/eval_jaxpr/mul | solution.py:26
  351.6 23.2 %mul.74 = f32[4608,36,36]{0,2,1:T(8,128)} reshape(f32[4608,1296]{0,1:T(8,128)} %fusion.18) | data formatting | bytes 47775744 | tf_op jit(solution)/shard_map/while/body/eval_jaxpr/mul | solution.py:26
  395.3 23.2 %mul.74 = f32[4608,36,36]{0,2,1:T(8,128)} reshape(f32[4608,1296]{0,1:T(8,128)} %fusion.18) | data formatting | bytes 47775744 | tf_op jit(solution)/shard_map/while/body/eval_jaxpr/mul | solution.py:26
  439.1 23.2 %mul.74 = f32[4608,36,36]{0,2,1:T(8,128)} reshape(f32[4608,1296]{0,1:T(8,128)} %fusion.18) | data formatting | bytes 47775744 | tf_op jit(solution)/shard_map/while/body/eval_jaxpr/mul | solution.py:26
  462.2 9.9 reduce_sum.46
  482.8 23.2 %mul.74 = f32[4608,36,36]{0,2,1:T(8,128)} reshape(f32[4608,1296]{0,1:T(8,128)} %fusion.18) | data formatting | bytes 47775744 | tf_op jit(solution)/shard_map/while/body/eval_jaxpr/mul | solution.py:26
  506.0 9.9 reduce_sum.46
  534.0 33.8 %psum.35 = f32[8,36]{1,0:T(8,128)S(1)} all-reduce(f32[8,36]{1,0:T(8,128)S(1)} %reduce_sum.39), channel_id=1, replica_groups=mesh['pb'=64,'br'=4] {'br'}, use_global_device_ids=true, to_apply=%region_4.5 | all-reduce | flops 288 | bytes 2304 | tf_op jit(solution)/shard_map/psum | solution.py:36
  567.9 147.9 %all_gather.10 = f32[512,9]{1,0:T(8,128)S(1)} all-gather(f32[8,9]{1,0:T(8,128)S(1)} %dynamic-slice_divide_fusion), channel_id=1, replica_groups=mesh['pb'=64,'br'=4] {'pb'}, dimensions={0}, use_global_device_ids=true | all-gather | bytes 18720 | tf_op jit(solution)/shard_map/all_gather | solution.py:41
  715.9 14.1 %gather_fusion = f32[4096,9]{1,0:T(8,128)} fusion(f32[512,9]{1,0:T(8,128)S(1)} %all_gather.10, s32[4096]{0:T(1024)S(1)} %broadcast_clamp_fusion), kind=kCustom, calls=%fused_computation | custom fusion | bytes 311296 | tf_op jit(solution)/shard_map/gather | solution.py:65
  732.5 11.1 %fusion.6 = f32[8,1,36,1]{2,1,0,3:T(1,128)S(1)} fusion(f32[9,512,8,1]{1,3,2,0:T(1,128)S(1)} %copy.15, f32[9,512,8,36]{1,0,3,2:T(8,128)} %bitcast.51), kind=kOutput, calls=%fused_computation.11 | convolution fusion | flops 15925248 | bytes 5457024 | tf_op jit(solution)/shard_map/abqs,abq->qs/dot_general | solution.py:69
  743.6 33.2 %psum.36 = f32[8,36]{1,0:T(8,128)S(1)} all-reduce(f32[8,36]{1,0:T(8,128)S(1)} %bitcast.60), channel_id=1, replica_groups=mesh['pb'=64,'br'=4] {'br'}, use_global_device_ids=true, to_apply=%region_5.6 | all-reduce | flops 288 | bytes 2304 | tf_op jit(solution)/shard_map/psum | solution.py:36
  776.9 149.5 %all_gather.11 = f32[512,9]{1,0:T(8,128)S(1)} all-gather(f32[8,9]{1,0:T(8,128)S(1)} %add_divide_fusion.1), channel_id=1, replica_groups=mesh['pb'=64,'br'=4] {'pb'}, dimensions={0}, use_global_device_ids=true | all-gather | bytes 18720 | tf_op jit(solution)/shard_map/all_gather | solution.py:41
  926.4 14.1 %gather_fusion.1 = f32[4096,9]{1,0:T(8,128)} fusion(f32[512,9]{1,0:T(8,128)S(1)} %all_gather.11, s32[4096]{0:T(1024)S(1)} %broadcast_clamp_fusion), kind=kCustom, calls=%fused_computation.1 | custom fusion | bytes 311296 | tf_op jit(solution)/shard_map/gather | solution.py:65
  943.0 11.1 %fusion.4 = f32[8,1,36,1]{2,1,0,3:T(1,128)S(1)} fusion(f32[9,512,8,1]{1,3,2,0:T(1,128)S(1)} %copy.17, f32[9,512,8,36]{1,0,3,2:T(8,128)} %bitcast.52), kind=kOutput, calls=%fused_computation.9 | convolution fusion | flops 15925248 | bytes 5457024 | tf_op jit(solution)/shard_map/abqs,abq->qs/dot_general | solution.py:69
  954.2 33.4 %psum.37 = f32[8,36]{1,0:T(8,128)S(1)} all-reduce(f32[8,36]{1,0:T(8,128)S(1)} %bitcast.59), channel_id=1, replica_groups=mesh['pb'=64,'br'=4] {'br'}, use_global_device_ids=true, to_apply=%region_6.7 | all-reduce | flops 288 | bytes 2304 | tf_op jit(solution)/shard_map/psum | solution.py:36
  990.1 73.6 %all-reduce = (f32[1]{0:T(128)}, f32[1]{0:T(128)}) all-reduce(f32[1]{0:T(128)} %bitcast.20, f32[1]{0:T(128)} %bitcast.19), channel_id=1, replica_groups=mesh['pb'=64,'br'=4] {'pb','br'}, use_global_device_ids=true, to_apply=%region_10.11 | all-reduce | flops 2 | bytes 16 | tf_op jit(solution)/shard_map/psum | solution.py:73
  (45 shorter events, 152.8 us)
Async XLA Ops:
  516.8 7.2 copy-start
  524.1 43.8 %copy-start.1 = (f32[8,9]{1,0:T(8,128)S(1)}, f32[8,9]{1,0:T(8,128)}, u32[]{:S(2)}) copy-start(f32[8,9]{1,0:T(8,128)} %param.12) | copy-start | bytes 868
  524.1 191.8 %copy-start.2 = (s32[8,512]{1,0:T(8,128)S(1)}, s32[8,512]{1,0:T(8,128)}, u32[]{:S(2)}) copy-start(s32[8,512]{1,0:T(8,128)} %param.11) | copy-start | bytes 49156
  940.4 47.1 %copy-start.3 = (f32[8,9]{1,0:T(8,128)S(1)}, f32[8,9]{1,0:T(8,128)}, u32[]{:S(2)}) copy-start(f32[8,9]{1,0:T(8,128)} %param.13) | copy-start | bytes 868
where the time goes:
time: 1070 us
  blocking collectives  635 us (59%)
  local copies, waits for them, and re-layouts  232 us (22%)
  matrix products  99.9 us (9%)
  other arithmetic  96.2 us (9%)
    all_gather x2, blocking collectives, full_deviation(): return lax.all_gather(deviation, 'pb', axis=0, tiled=True)  297 us
    mul x8, local copies, waits for them, and re-layouts, per_point(): return jnp.sum(amplitude * amplitude, axis=2)  185 us
    all_gather x1, blocking collectives, on_device(): lax.all_gather(polarization, 'pb', axis=1, tiled=True)  164 us
    psum x3, blocking collectives, branch_total(): summed = lax.psum(partial_sum, 'br')  100 us
    reduce_sum x8, other arithmetic, per_point(): return jnp.sum(amplitude * amplitude, axis=2)  79.6 us
    dot_general x8, matrix products, per_point(): jnp.dot(flat_rows, const_block, preferred_element_type=jnp.float32)  77.6 us
    psum x1, blocking collectives, on_device(): kappas.append(lax.psum(kappa_term, ('pb', 'br')))  73.6 us
    gather x2, local copies, waits for them, and re-layouts, on_device(): partner_value = deviation_all[partner]  28.1 us

commit v1 on v0

--- a/solution.py
+++ b/solution.py
@@ -37,8 +37,18 @@
     return lax.dynamic_slice_in_dim(summed, lax.axis_index("br") * own_count, own_count, 1)
 
 
+def gather_pb(block, axis):
+    count = lax.axis_size("pb")
+    copies = jnp.broadcast_to(block[None], (count,) + block.shape)
+    got = lax.all_to_all(copies, "pb", 0, 0, tiled=True)
+    got = jnp.moveaxis(got, 0, axis)
+    shape = list(block.shape)
+    shape[axis] *= count
+    return got.reshape(shape)
+
+
 def full_deviation(deviation):
-    return lax.all_gather(deviation, "pb", axis=0, tiled=True)
+    return gather_pb(deviation, 0)
 
 
 def on_device(bloch_const, polarization, delta_weight, partner, velocity, capacity):
@@ -52,9 +62,7 @@
     folder = partial(
         coupling_fold, const_blocks=const_blocks, delta_local=delta_weight, inv_count=inv_count
     )
-    coupling = folder(
-        zero_start, lax.all_gather(polarization, "pb", axis=1, tiled=True), jnp.int32(0)
-    )
+    coupling = folder(zero_start, gather_pb(polarization, 1), jnp.int32(0))
     coupling = coupling.reshape(own_count, total_points, local_points, all_branches)
     rate_total = branch_total(jnp.sum(coupling, axis=(0, 1)))
     deviation = velocity / rate_total
@@ -69,9 +77,11 @@
         spread = jnp.einsum("abqs,abq->qs", coupling, combined, precision=lax.Precision.HIGHEST)
         spread = branch_total(spread)
         deviation = (velocity + 0.5 * spread) / rate_total
-        kappa_term = jnp.sum(heat_weight * deviation) * inv_count
-        kappas.append(lax.psum(kappa_term, ("pb", "br")))
-    kappa = jnp.stack(kappas)
+        kappas.append(jnp.sum(heat_weight * deviation))
+    axes = ("pb", "br")
+    devices = lax.axis_size(axes)
+    partials = jnp.broadcast_to(jnp.stack(kappas)[None], (devices, ITERS))
+    kappa = jnp.sum(lax.all_to_all(partials, axes, 0, 0, tiled=True), axis=0) * inv_count
     return (deviation, kappa)
 
 

time: 1070 us -> 544 us (0.51)
  blocking collectives: 635 us -> 59.8 us
  waiting for transfers between devices: 0 us -> 21.9 us
  starting transfers between devices: 0 us -> 21 us
    all_gather x3 -> x0, blocking collectives: 461 us -> none  [the longest x2 297 us: full_deviation(): return lax.all_gather(deviation, 'pb', axis=0, tiled=True)]
    psum x3, blocking collectives: 100 us -> 24.7 us  [branch_total(): summed = lax.psum(partial_sum, 'br')]
    psum x1 -> x0, blocking collectives: 73.6 us -> none  [on_device(): kappas.append(lax.psum(kappa_term, ('pb', 'br')))]
    all_to_all x0 -> x2, blocking collectives: none -> 35.1 us  [the longest x1 18.4 us: on_device(): lax.all_to_all(partials, axes, 0, 0, tiled=True)]
    all_to_all x0 -> x2, waiting for transfers between devices: none -> 21.9 us  [gather_pb(): got = lax.all_to_all(copies, 'pb', 0, 0, tiled=True)]
    all_to_all x0 -> x2, starting transfers between devices: none -> 21 us  [gather_pb(): got = lax.all_to_all(copies, 'pb', 0, 0, tiled=True)]
  transfers between devices with their start and end apart: 0 -> 2, of which waited for: 0 -> 2; matrix products, arithmetic and copies ran while one was open for 0% -> 1% of each run, Pallas kernels for 0% -> 0%
where the time goes in v1:
time: 544 us; the launch traced here: 538 us
  local copies, waits for them, and re-layouts  238 us (44%)
  matrix products  99.9 us (18%)
  other arithmetic  96.7 us (18%)
  blocking collectives  59.8 us (11%)
  waiting for transfers between devices  21.9 us (4%)
  starting transfers between devices  21 us (4%)
    mul x8, local copies, waits for them, and re-layouts, per_point(): return jnp.sum(amplitude * amplitude, axis=2)  185 us
    reduce_sum x8, other arithmetic, per_point(): return jnp.sum(amplitude * amplitude, axis=2)  79.6 us
    dot_general x8, matrix products, per_point(): jnp.dot(flat_rows, const_block, preferred_element_type=jnp.float32)  77.6 us
    gather x2, local copies, waits for them, and re-layouts, on_device(): partner_value = deviation_all[partner]  28.1 us
    psum x3, blocking collectives, branch_total(): summed = lax.psum(partial_sum, 'br')  24.7 us
    dot_general x2, matrix products, on_device(): jnp.einsum('abqs,abq->qs', coupling, combined, precision=lax.Precision.HI...  22.3 us
    all_to_all x2, waiting for transfers between devices, gather_pb(): got = lax.all_to_all(copies, 'pb', 0, 0, tiled=True)  21.9 us
    all_to_all x2, starting transfers between devices, gather_pb(): got = lax.all_to_all(copies, 'pb', 0, 0, tiled=True)  21 us
  transfers between devices with their start and end apart: 2, of which 2 were waited for; matrix products, arithmetic and copies ran while one was open for 1% of the time, Pallas kernels for 0%

profile of v1, /device:TPU:1, one launch (start us, length us, event | category | flops | bytes accessed | tf_op | source)
XLA Modules:
  0.0 538.5 jit_solution(306247899662813096)
XLA Ops:
  4.0 15.1 %all-to-all-start = ((bf16[64,2,1296]{2,1,0:T(2,128)(2,1)}), bf16[64,2,1296]{2,1,0:T(2,128)(2,1)S(1)}, u32[]{:S(2)}, u32[]{:S(2)}) async-start(bf16[64,2,1296]{2,1,0:T(2,128)(2,1)} %reshape.58), calls=%async_computation | async-start | bytes 720896 | tf_op jit(solution)/shard_map/all_to_all | solution.py:43
  22.2 10.0 %all-to-all-done = bf16[64,2,1296]{2,1,0:T(2,128)(2,1)S(1)} async-done(((bf16[64,2,1296]{2,1,0:T(2,128)(2,1)}), bf16[64,2,1296]{2,1,0:T(2,128)(2,1)S(1)}, u32[]{:S(2)}, u32[]{:S(2)}) %all-to-all-start) | async-done | bytes 331808 | tf_op jit(solution)/shard_map/all_to_all | solution.py:43
  33.6 350.0 %while.10 = (s32[]{:T(128)}, f32[8,4608,36]{1,2,0:T(8,128)}, bf16[8,36,1296]{2,1,0:T(8,128)(2,1)S(1)}, bf16[4608,36]{1,0:T(8,128)(2,1)S(1)}, s32[]{:T(128)}, /*index=5*/f32[]{:T(128)}) while((s32[]{:T(128)}, f32[8,4608,36]{1,2,0:T(8,128)}, bf16[8,36,1296]{2,1,0:T(8,128)(2,1)S(1)}, bf16[4608,36]{1,0:T(8,128)(2,1)S(1)}, s32[]{:T(128)}, ...), condition=%wide.region_2.3_spmd, body=%wide.region_0.2_spmd.sunk | while | flops 441759744 | bytes 98908744 | solution.py:28
  43.4 23.2 %mul.71 = f32[4608,36,36]{0,2,1:T(8,128)} reshape(f32[4608,1296]{0,1:T(8,128)} %fusion.18) | data formatting | bytes 47775744 | tf_op jit(solution)/shard_map/while/body/eval_jaxpr/mul | solution.py:26
  66.5 9.9 %reduce_sum.56 = f32[4608,36]{0,1:T(8,128)S(1)} reduce(f32[4608,36,36]{0,2,1:T(8,128)} %mul.71, f32[]{:T(128)} %constant.3.clone.1..sunk), dimensions={2}, to_apply=%region_1.1 | reduce | flops 5806080 | bytes 24551428 | tf_op jit(solution)/shard_map/while/body/eval_jaxpr/reduce_sum | solution.py:26
  87.1 23.2 %mul.71 = f32[4608,36,36]{0,2,1:T(8,128)} reshape(f32[4608,1296]{0,1:T(8,128)} %fusion.18) | data formatting | bytes 47775744 | tf_op jit(solution)/shard_map/while/body/eval_jaxpr/mul | solution.py:26
  110.2 9.9 %reduce_sum.56 = f32[4608,36]{0,1:T(8,128)S(1)} reduce(f32[4608,36,36]{0,2,1:T(8,128)} %mul.71, f32[]{:T(128)} %constant.3.clone.1..sunk), dimensions={2}, to_apply=%region_1.1 | reduce | flops 5806080 | bytes 24551428 | tf_op jit(solution)/shard_map/while/body/eval_jaxpr/reduce_sum | solution.py:26
  130.8 23.2 %mul.71 = f32[4608,36,36]{0,2,1:T(8,128)} reshape(f32[4608,1296]{0,1:T(8,128)} %fusion.18) | data formatting | bytes 47775744 | tf_op jit(solution)/shard_map/while/body/eval_jaxpr/mul | solution.py:26
  154.0 9.9 %reduce_sum.56 = f32[4608,36]{0,1:T(8,128)S(1)} reduce(f32[4608,36,36]{0,2,1:T(8,128)} %mul.71, f32[]{:T(128)} %constant.3.clone.1..sunk), dimensions={2}, to_apply=%region_1.1 | reduce | flops 5806080 | bytes 24551428 | tf_op jit(solution)/shard_map/while/body/eval_jaxpr/reduce_sum | solution.py:26
  174.6 23.2 %mul.71 = f32[4608,36,36]{0,2,1:T(8,128)} reshape(f32[4608,1296]{0,1:T(8,128)} %fusion.18) | data formatting | bytes 47775744 | tf_op jit(solution)/shard_map/while/body/eval_jaxpr/mul | solution.py:26
  197.7 9.9 %reduce_sum.56 = f32[4608,36]{0,1:T(8,128)S(1)} reduce(f32[4608,36,36]{0,2,1:T(8,128)} %mul.71, f32[]{:T(128)} %constant.3.clone.1..sunk), dimensions={2}, to_apply=%region_1.1 | reduce | flops 5806080 | bytes 24551428 | tf_op jit(solution)/shard_map/while/body/eval_jaxpr/reduce_sum | solution.py:26
  218.3 23.2 %mul.71 = f32[4608,36,36]{0,2,1:T(8,128)} reshape(f32[4608,1296]{0,1:T(8,128)} %fusion.18) | data formatting | bytes 47775744 | tf_op jit(solution)/shard_map/while/body/eval_jaxpr/mul | solution.py:26
  241.5 9.9 %reduce_sum.56 = f32[4608,36]{0,1:T(8,128)S(1)} reduce(f32[4608,36,36]{0,2,1:T(8,128)} %mul.71, f32[]{:T(128)} %constant.3.clone.1..sunk), dimensions={2}, to_apply=%region_1.1 | reduce | flops 5806080 | bytes 24551428 | tf_op jit(solution)/shard_map/while/body/eval_jaxpr/reduce_sum | solution.py:26
  262.1 23.2 %mul.71 = f32[4608,36,36]{0,2,1:T(8,128)} reshape(f32[4608,1296]{0,1:T(8,128)} %fusion.18) | data formatting | bytes 47775744 | tf_op jit(solution)/shard_map/while/body/eval_jaxpr/mul | solution.py:26
  285.2 9.9 %reduce_sum.56 = f32[4608,36]{0,1:T(8,128)S(1)} reduce(f32[4608,36,36]{0,2,1:T(8,128)} %mul.71, f32[]{:T(128)} %constant.3.clone.1..sunk), dimensions={2}, to_apply=%region_1.1 | reduce | flops 5806080 | bytes 24551428 | tf_op jit(solution)/shard_map/while/body/eval_jaxpr/reduce_sum | solution.py:26
  305.8 23.2 %mul.71 = f32[4608,36,36]{0,2,1:T(8,128)} reshape(f32[4608,1296]{0,1:T(8,128)} %fusion.18) | data formatting | bytes 47775744 | tf_op jit(solution)/shard_map/while/body/eval_jaxpr/mul | solution.py:26
  349.5 23.2 %mul.71 = f32[4608,36,36]{0,2,1:T(8,128)} reshape(f32[4608,1296]{0,1:T(8,128)} %fusion.18) | data formatting | bytes 47775744 | tf_op jit(solution)/shard_map/while/body/eval_jaxpr/mul | solution.py:26
  415.7 11.8 %all-to-all-done.1 = f32[64,8,9]{2,1,0:T(8,128)S(1)} async-done(((f32[64,8,9]{2,1,0:T(8,128)}), f32[64,8,9]{2,1,0:T(8,128)S(1)}, u32[]{:S(2)}, u32[]{:S(2)}) %all-to-all-start.1) | async-done | bytes 18464 | tf_op jit(solution)/shard_map/all_to_all | solution.py:43
  427.5 14.1 %gather_fusion = f32[4096,9]{1,0:T(8,128)} fusion(f32[512,9]{1,0:T(8,128)S(1)} %bitcast.54, s32[4096]{0:T(1024)S(1)} %broadcast_clamp_fusion), kind=kCustom, calls=%fused_computation | custom fusion | bytes 311296 | tf_op jit(solution)/shard_map/gather | solution.py:73
  444.2 11.1 %fusion.6 = f32[8,1,36,1]{2,1,0,3:T(1,128)S(1)} fusion(f32[9,512,8,1]{1,3,2,0:T(1,128)S(1)} %copy.28, f32[9,512,8,36]{1,0,3,2:T(8,128)} %bitcast.58), kind=kOutput, calls=%fused_computation.11 | convolution fusion | flops 15925248 | bytes 5457024 | tf_op jit(solution)/shard_map/abqs,abq->qs/dot_general | solution.py:77
  463.7 16.7 %all_to_all.21 = f32[64,8,9]{2,1,0:T(8,128)S(1)} all-to-all(f32[64,8,9]{2,1,0:T(8,128)S(1)} %broadcast_in_dim.20), channel_id=1, replica_groups=mesh['pb'=64,'br'=4] {'pb'}, dimensions={0} | all-to-all | bytes 36864 | tf_op jit(solution)/shard_map/all_to_all | solution.py:43
  480.4 14.1 %gather_fusion.1 = f32[4096,9]{1,0:T(8,128)} fusion(f32[512,9]{1,0:T(8,128)S(1)} %bitcast.56, s32[4096]{0:T(1024)S(1)} %broadcast_clamp_fusion), kind=kCustom, calls=%fused_computation.1 | custom fusion | bytes 311296 | tf_op jit(solution)/shard_map/gather | solution.py:73
  497.0 11.1 %fusion.4 = f32[8,1,36,1]{2,1,0,3:T(1,128)S(1)} fusion(f32[9,512,8,1]{1,3,2,0:T(1,128)S(1)} %copy.30, f32[9,512,8,36]{1,0,3,2:T(8,128)} %bitcast.59), kind=kOutput, calls=%fused_computation.9 | convolution fusion | flops 15925248 | bytes 5457024 | tf_op jit(solution)/shard_map/abqs,abq->qs/dot_general | solution.py:77
  519.2 18.4 %all_to_all.22 = f32[256,1,2]{2,1,0:T(1,128)S(1)} all-to-all(f32[256,1,2]{2,1,0:T(1,128)S(1)} %broadcast_in_dim.21), channel_id=1, replica_groups=mesh['pb'=64,'br'=4] {'pb','br'}, dimensions={0} | all-to-all | bytes 4096 | tf_op jit(solution)/shard_map/all_to_all | solution.py:84
  (58 shorter events, 170.2 us)
Async XLA Ops:
  0.6 20.9 %copy-start.3 = (s32[8,512]{1,0:T(8,128)S(1)}, s32[8,512]{1,0:T(8,128)}, u32[]{:S(2)}) copy-start(s32[8,512]{1,0:T(8,128)} %param.11) | copy-start | bytes 49156
  4.0 28.2 %all-to-all-start = ((bf16[64,2,1296]{2,1,0:T(2,128)(2,1)}), bf16[64,2,1296]{2,1,0:T(2,128)(2,1)S(1)}, u32[]{:S(2)}, u32[]{:S(2)}) async-start(bf16[64,2,1296]{2,1,0:T(2,128)(2,1)} %reshape.58), calls=%async_computation | async-start | bytes 720896 | tf_op jit(solution)/shard_map/all_to_all | solution.py:43
  383.6 7.2 %copy-start = (bf16[9,512,288]{1,2,0:T(8,128)(2,1)S(1)}, bf16[9,512,288]{1,2,0:T(8,128)(2,1)}, u32[]{:S(2)}) copy-start(bf16[9,512,288]{1,2,0:T(8,128)(2,1)} %param.10) | copy-start | bytes 7962628
  390.8 18.2 %copy-start.2 = (f32[8,9]{1,0:T(8,128)S(1)}, f32[8,9]{1,0:T(8,128)}, u32[]{:S(2)}) copy-start(f32[8,9]{1,0:T(8,128)} %param.12) | copy-start | bytes 868
  390.8 24.9 %copy-start.1 = (s32[1,4,8,128]{3,1,2,0:T(4,128)S(1)}, s32[1,4,8,128]{3,1,2,0:T(4,128)}, u32[]{:S(2)}) copy-start(s32[1,4,8,128]{3,1,2,0:T(4,128)} %copy.34) | copy-start | bytes 49156
  409.8 17.7 %all-to-all-start.1 = ((f32[64,8,9]{2,1,0:T(8,128)}), f32[64,8,9]{2,1,0:T(8,128)S(1)}, u32[]{:S(2)}, u32[]{:S(2)}) async-start(f32[64,8,9]{2,1,0:T(8,128)} %broadcast_in_dim.18), calls=%async_computation.1 | async-start | bytes 524288 | tf_op jit(solution)/shard_map/all_to_all | solution.py:43
  494.4 22.0 %copy-start.4 = (f32[8,9]{1,0:T(8,128)S(1)}, f32[8,9]{1,0:T(8,128)}, u32[]{:S(2)}) copy-start(f32[8,9]{1,0:T(8,128)} %param.13) | copy-start | bytes 868

commit v2 on v1

v2 whole, which is shorter than its diff:
```python
from functools import partial

import jax
import jax.numpy as jnp
from jax import lax
from jax.experimental import pallas as pl
from jax.experimental.pallas import tpu as pltpu
from jax.sharding import PartitionSpec as P

ITERS = 2


def coupling_kernel(bt_ref, pt_ref, dw_ref, out_ref, acc_ref, *, inv_count):
    pt = pt_ref[...]
    acc_ref[...] = jnp.zeros(acc_ref.shape, jnp.float32)

    def body(n, carry):
        amp = jnp.dot(bt_ref[n], pt, preferred_element_type=jnp.float32)
        acc_ref[...] += amp * amp
        return carry

    lax.fori_loop(0, bt_ref.shape[0], body, 0)
    out_ref[...] = acc_ref[...] * dw_ref[...].astype(jnp.float32) * inv_count


def coupling_call(bt, pt, dw, inv_count, tile=512):
    comps, rows, m = bt.shape
    cols = pt.shape[1]
    return pl.pallas_call(
        partial(coupling_kernel, inv_count=inv_count),
        grid=(cols // tile,),
        in_specs=[
            pl.BlockSpec((comps, rows, m), lambda i: (0, 0, 0)),
            pl.BlockSpec((m, tile), lambda i: (0, i)),
            pl.BlockSpec((rows, tile), lambda i: (0, i)),
        ],
        out_specs=pl.BlockSpec((rows, tile), lambda i: (0, i)),
        out_shape=jax.ShapeDtypeStruct((rows, cols), jnp.float32),
        scratch_shapes=[pltpu.VMEM((rows, tile), jnp.float32)],
    )(bt, pt, dw)


def branch_total(partial_sum):
    own_count = partial_sum.shape[1] // lax.axis_size("br")
    summed = lax.psum(partial_sum, "br")
    return lax.dynamic_slice_in_dim(summed, lax.axis_index("br") * own_count, own_count, 1)


def gather_pb(block, axis):
    count = lax.axis_size("pb")
    copies = jnp.broadcast_to(block[None], (count,) + block.shape)
    got = lax.all_to_all(copies, "pb", 0, 0, tiled=True)
    got = jnp.moveaxis(got, 0, axis)
    shape = list(block.shape)
    shape[axis] *= count
    return got.reshape(shape)


def full_deviation(deviation):
    return gather_pb(deviation, 0)


def on_device(bloch_const, polarization, delta_weight, partner, velocity, capacity):
    local_points = velocity.shape[0]
    own_count = velocity.shape[1]
    all_branches = own_count * lax.axis_size("br")
    total_points = polarization.shape[1] * lax.axis_size("pb")
    inv_count = 1.0 / (total_points * all_branches)
    components = bloch_const.shape[0]
    bt = bloch_const.reshape(components, local_points, all_branches, -1)
    bt = jnp.transpose(bt, (3, 1, 2, 0)).reshape(-1, local_points * all_branches, components)
    pol_all = gather_pb(polarization, 1)
    pt = jnp.transpose(pol_all, (2, 0, 1)).reshape(components, own_count * total_points)
    dw = jnp.transpose(delta_weight.reshape(own_count * total_points, -1))
    coupling_t = coupling_call(bt, pt, dw, inv_count)
    coupling = coupling_t.reshape(local_points, all_branches, own_count * total_points)
    rate_total = branch_total(jnp.sum(coupling, axis=2))
    deviation = velocity / rate_total
    heat_weight = capacity * velocity
    kappas = []
    for sweep_index in range(ITERS):
        deviation_all = full_deviation(deviation)
        partner_value = deviation_all[partner]
        combined = jnp.transpose(deviation_all)[None] + jnp.transpose(partner_value, (0, 2, 1))
        combined = combined.reshape(local_points, 1, -1)
        spread = jnp.sum(coupling * combined, axis=2)
        spread = branch_total(spread)
        deviation = (velocity + 0.5 * spread) / rate_total
        kappas.append(jnp.sum(heat_weight * deviation))
    axes = ("pb", "br")
    devices = lax.axis_size(axes)
    partials = jnp.broadcast_to(jnp.stack(kappas)[None], (devices, ITERS))
    kappa = jnp.sum(lax.all_to_all(partials, axes, 0, 0, tiled=True), axis=0) * inv_count
    return (deviation, kappa)


def solution(mesh):
    in_specs = (
        P(None, "pb"),
        P("br", "pb", None),
        P("br", None, "pb"),
        P("pb", None),
        P("pb", "br"),
        P("pb", "br"),
    )
    out_specs = (P("pb", "br"), P())
    return jax.shard_map(
        on_device, mesh=mesh, in_specs=in_specs, out_specs=out_specs, check_vma=False
    )
```

time: 544 us -> 254 us (0.47)
  local copies, waits for them, and re-layouts: 238 us -> 67.3 us
  matrix products: 99.9 us -> 0 us
  other arithmetic: 96.7 us -> 15.9 us
  Pallas kernels: 0 us -> 72.1 us
  waiting for transfers between devices: 21.9 us -> 11.8 us
  starting transfers between devices: 21 us -> 27.7 us
    mul x8 -> x4, local copies, waits for them, and re-layouts: 185 us -> 17.5 us  [on_device(): spread = jnp.sum(coupling * combined, axis=2)]
    dot_general x10 -> x0, matrix products: 99.9 us -> none  [the longest x8 77.6 us: per_point(): jnp.dot(flat_rows, const_block, preferred_element_type=jnp.float32)]
    reduce_sum x9 -> x3, other arithmetic: 89.5 us -> 12.2 us  [the longest x2 9.3 us: on_device(): spread = jnp.sum(coupling * combined, axis=2)]
    pallas_call x0 -> x1, Pallas kernels: none -> 72.1 us  [coupling_call(): pl.pallas_call(partial(coupling_kernel, inv_count=inv_count), grid=(cols...]
    all_to_all x2, waiting for transfers between devices: 21.9 us -> 11.8 us  [gather_pb(): got = lax.all_to_all(copies, 'pb', 0, 0, tiled=True)]
    reshape x1 -> x5, local copies, waits for them, and re-layouts: 7.22 us -> 16.3 us  [the longest x2 7.84 us: on_device(): jnp.transpose(bt, (3, 1, 2, 0))]
    dynamic_update_slice x8 -> x0, local copies, waits for them, and re-layouts: 7.43 us -> none  [coupling_fold(): squared = lax.map(per_point, const_blocks)]
    all_to_all x2, starting transfers between devices: 21 us -> 27.7 us  [gather_pb(): got = lax.all_to_all(copies, 'pb', 0, 0, tiled=True)]
  transfers between devices with their start and end apart: 2 -> 2, of which waited for: 2 -> 1; matrix products, arithmetic and copies ran while one was open for 1% -> 7% of each run, Pallas kernels for 0% -> 0%
where the time goes in v2:
time: 254 us; the launch traced here: 253 us
  Pallas kernels  72.1 us (28%)
  local copies, waits for them, and re-layouts  67.3 us (26%)
  blocking collectives  57.7 us (23%)
  starting transfers between devices  27.7 us (11%)
  other arithmetic  15.9 us (6%)
  waiting for transfers between devices  11.8 us (5%)
    pallas_call x1, Pallas kernels, coupling_call(): pl.pallas_call(partial(coupling_kernel, inv_count=inv_count), grid=(cols...  72.1 us
    all_to_all x2, starting transfers between devices, gather_pb(): got = lax.all_to_all(copies, 'pb', 0, 0, tiled=True)  27.7 us
    gather x4, local copies, waits for them, and re-layouts, on_device(): partner_value = deviation_all[partner]  22.8 us
    psum x3, blocking collectives, branch_total(): summed = lax.psum(partial_sum, 'br')  22.6 us
    all_to_all x1, blocking collectives, on_device(): lax.all_to_all(partials, axes, 0, 0, tiled=True)  18.4 us
    mul x4, local copies, waits for them, and re-layouts, on_device(): spread = jnp.sum(coupling * combined, axis=2)  17.5 us
    all_to_all x1, blocking collectives, gather_pb(): got = lax.all_to_all(copies, 'pb', 0, 0, tiled=True)  16.7 us
    all_to_all x2, waiting for transfers between devices, gather_pb(): got = lax.all_to_all(copies, 'pb', 0, 0, tiled=True)  11.8 us
  transfers between devices with their start and end apart: 2, of which 1 were waited for; matrix products, arithmetic and copies ran while one was open for 7% of the time, Pallas kernels for 0%

profile of v2, /device:TPU:1, one launch (start us, length us, event | category | flops | bytes accessed | tf_op | source)
XLA Modules:
  0.0 253.4 jit_solution(22769922082733875)
XLA Ops:
  1.5 2.5 reshape.74
  4.0 15.3 %all-to-all-start = ((bf16[64,2,1296]{2,1,0:T(2,128)(2,1)}), bf16[64,2,1296]{2,1,0:T(2,128)(2,1)}, u32[]{:S(2)}, u32[]{:S(2)}) async-start(bf16[64,2,1296]{2,1,0:T(2,128)(2,1)} %reshape.74), calls=%async_computation | async-start | bytes 720896 | tf_op jit(solution)/shard_map/all_to_all | solution.py:52
  19.4 4.3 %reshape.46 = bf16[36,8,36,36]{3,2,1,0:T(8,128)(2,1)S(1)} reshape(bf16[36,10368]{1,0:T(8,128)(2,1)} %param.6) | data formatting | bytes 1492992 | tf_op jit(solution)/shard_map/reshape | solution.py:70
  23.7 2.5 reshape.73
  26.2 5.3 %copy.45.bt_ref = bf16[36,288,36]{2,1,0:T(8,128)(2,1)} copy(bf16[36,288,36]{0,1,2:T(8,128)(2,1)} %reshape.73) | data formatting | bytes 1492992 | tf_op jit(solution)/shard_map/reshape | solution.py:71
  31.6 3.5 %copy.43 = bf16[9,512,288]{2,1,0:T(8,128)(2,1)S(1)} copy(bf16[9,512,288]{1,2,0:T(8,128)(2,1)} %param.8) | data formatting | bytes 5308416 | tf_op args[2]
  35.0 2.9 %copy.44 = bf16[4608,288]{0,1:T(8,128)(2,1)} copy(bf16[4608,288]{1,0:T(8,128)(2,1)S(1)} %bitcast.34) | data formatting | bytes 5308416 | tf_op jit(solution)/shard_map/reshape | solution.py:74
  41.8 72.1 %shard_map.77 = f32[288,4608]{1,0:T(8,128)} custom-call(bf16[36,288,36]{2,1,0:T(8,128)(2,1)} %copy.45.bt_ref, bf16[36,4608]{1,0:T(8,128)(2,1)} %copy.53.pt_ref, bf16[288,4608]{1,0:T(8,128)(2,1)} %bitcast.36), custom_call_target="tpu_custom_call" | custom-call | tf_op jit(solution)/shard_map/pallas_call | solution.py:29
  113.8 2.9 %reduce_sum.60 = f32[288]{0:T(512)S(1)} reduce(f32[288,4608]{1,0:T(8,128)} %shard_map.77, f32[]{:T(128)} %constant.8.clone.1), dimensions={1}, to_apply=%region_0.0 | reduce | flops 1326816 | bytes 5309572 | tf_op jit(solution)/shard_map/reduce_sum | solution.py:77
  116.8 6.0 %psum.21 = f32[8,36]{1,0:T(8,128)S(1)} all-reduce(f32[8,36]{1,0:T(8,128)S(1)} %reduce_sum.61), channel_id=1, replica_groups=mesh['pb'=64,'br'=4] {'br'}, use_global_device_ids=true, to_apply=%region_1.0 | all-reduce | flops 288 | bytes 2304 | tf_op jit(solution)/shard_map/psum | solution.py:45
  123.5 12.4 %all-to-all-start.1 = ((f32[64,8,9]{2,1,0:T(8,128)}), f32[64,8,9]{2,1,0:T(8,128)S(1)}, u32[]{:S(2)}, u32[]{:S(2)}) async-start(f32[64,8,9]{2,1,0:T(8,128)} %broadcast_in_dim.11), calls=%async_computation.1 | async-start | bytes 524288 | tf_op jit(solution)/shard_map/all_to_all | solution.py:52
  135.9 11.8 %all-to-all-done.1 = f32[64,8,9]{2,1,0:T(8,128)S(1)} async-done(((f32[64,8,9]{2,1,0:T(8,128)}), f32[64,8,9]{2,1,0:T(8,128)S(1)}, u32[]{:S(2)}, u32[]{:S(2)}) %all-to-all-start.1) | async-done | bytes 18464 | tf_op jit(solution)/shard_map/all_to_all | solution.py:52
  147.9 10.8 %gather_fusion = f32[4096,9]{1,0:T(8,128)S(1)} fusion(f32[512,9]{1,0:T(8,128)S(1)} %bitcast.31, s32[4096]{0:T(1024)S(1)} %broadcast_clamp_fusion), kind=kCustom, calls=%fused_computation | custom fusion | bytes 311296 | tf_op jit(solution)/shard_map/gather | solution.py:83
  159.3 3.2 %mul.51 = f32[8,36,4608]{2,1,0:T(8,128)} broadcast(f32[8,4608]{1,0:T(8,128)S(1)} %bitcast.41), dimensions={0,2} | broadcast | bytes 5455872 | tf_op jit(solution)/shard_map/mul | solution.py:86
  162.5 5.5 %mul.52 = f32[288,4608]{1,0:T(8,128)} reshape(f32[8,36,4608]{2,1,0:T(8,128)} %mul.51) | data formatting | bytes 10616832 | tf_op jit(solution)/shard_map/mul | solution.py:86
  168.1 4.6 %multiply_reduce_fusion.1 = f32[288]{0:T(512)S(1)} fusion(f32[288,4608]{1,0:T(8,128)} %shard_map.77, f32[288,4608]{1,0:T(8,128)} %mul.52), kind=kLoop, calls=%fused_computation.3 | loop fusion | flops 2653920 | bytes 10617984 | tf_op jit(solution)/shard_map/reduce_sum | solution.py:86
  172.8 8.4 %psum.22 = f32[8,36]{1,0:T(8,128)S(1)} all-reduce(f32[8,36]{1,0:T(8,128)S(1)} %reduce_sum.63), channel_id=1, replica_groups=mesh['pb'=64,'br'=4] {'br'}, use_global_device_ids=true, to_apply=%region_3.0 | all-reduce | flops 288 | bytes 2304 | tf_op jit(solution)/shard_map/psum | solution.py:45
  181.3 16.7 %all_to_all.21 = f32[64,8,9]{2,1,0:T(8,128)S(1)} all-to-all(f32[64,8,9]{2,1,0:T(8,128)S(1)} %broadcast_in_dim.13), channel_id=1, replica_groups=mesh['pb'=64,'br'=4] {'pb'}, dimensions={0} | all-to-all | bytes 36864 | tf_op jit(solution)/shard_map/all_to_all | solution.py:52
  198.1 10.8 %gather_fusion.1 = f32[4096,9]{1,0:T(8,128)S(1)} fusion(f32[512,9]{1,0:T(8,128)S(1)} %bitcast.33, s32[4096]{0:T(1024)S(1)} %broadcast_clamp_fusion), kind=kCustom, calls=%fused_computation.1 | custom fusion | bytes 311296 | tf_op jit(solution)/shard_map/gather | solution.py:83
  209.6 3.2 %mul.56 = f32[8,36,4608]{2,1,0:T(8,128)} broadcast(f32[8,4608]{1,0:T(8,128)S(1)} %bitcast.42), dimensions={0,2} | broadcast | bytes 5455872 | tf_op jit(solution)/shard_map/mul | solution.py:86
  212.8 5.5 %mul.57 = f32[288,4608]{1,0:T(8,128)} reshape(f32[8,36,4608]{2,1,0:T(8,128)} %mul.56) | data formatting | bytes 10616832 | tf_op jit(solution)/shard_map/mul | solution.py:86
  218.3 4.7 %multiply_reduce_fusion = f32[288]{0:T(512)S(1)} fusion(f32[288,4608]{1,0:T(8,128)} %shard_map.77, f32[288,4608]{1,0:T(8,128)} %mul.57), kind=kLoop, calls=%fused_computation.2 | loop fusion | flops 2653920 | bytes 10617984 | tf_op jit(solution)/shard_map/reduce_sum | solution.py:86
  223.1 8.2 %psum.23 = f32[8,36]{1,0:T(8,128)S(1)} all-reduce(f32[8,36]{1,0:T(8,128)S(1)} %reduce_sum.65), channel_id=1, replica_groups=mesh['pb'=64,'br'=4] {'br'}, use_global_device_ids=true, to_apply=%region_5.0 | all-reduce | flops 288 | bytes 2304 | tf_op jit(solution)/shard_map/psum | solution.py:45
  234.1 18.4 %all_to_all.22 = f32[256,1,2]{2,1,0:T(1,128)S(1)} all-to-all(f32[256,1,2]{2,1,0:T(1,128)S(1)} %broadcast_in_dim.14), channel_id=1, replica_groups=mesh['pb'=64,'br'=4] {'pb','br'}, dimensions={0} | all-to-all | bytes 4096 | tf_op jit(solution)/shard_map/all_to_all | solution.py:93
  (32 shorter events, 11.0 us)
Async XLA Ops:
  0.6 18.7 %copy-start.1 = (s32[8,512]{1,0:T(8,128)S(1)}, s32[8,512]{1,0:T(8,128)}, u32[]{:S(2)}) copy-start(s32[8,512]{1,0:T(8,128)} %param.9) | copy-start | bytes 49156
  4.0 34.0 %all-to-all-start = ((bf16[64,2,1296]{2,1,0:T(2,128)(2,1)}), bf16[64,2,1296]{2,1,0:T(2,128)(2,1)}, u32[]{:S(2)}, u32[]{:S(2)}) async-start(bf16[64,2,1296]{2,1,0:T(2,128)(2,1)} %reshape.74), calls=%async_computation | async-start | bytes 720896 | tf_op jit(solution)/shard_map/all_to_all | solution.py:52
  113.8 8.9 %copy-start = (f32[8,9]{1,0:T(8,128)S(1)}, f32[8,9]{1,0:T(8,128)}, u32[]{:S(2)}) copy-start(f32[8,9]{1,0:T(8,128)} %param.10) | copy-start | bytes 868
  123.5 24.2 %all-to-all-start.1 = ((f32[64,8,9]{2,1,0:T(8,128)}), f32[64,8,9]{2,1,0:T(8,128)S(1)}, u32[]{:S(2)}, u32[]{:S(2)}) async-start(f32[64,8,9]{2,1,0:T(8,128)} %broadcast_in_dim.11), calls=%async_computation.1 | async-start | bytes 524288 | tf_op jit(solution)/shard_map/all_to_all | solution.py:52
  218.3 13.0 %copy-start.2 = (f32[8,9]{1,0:T(8,128)S(1)}, f32[8,9]{1,0:T(8,128)}, u32[]{:S(2)}) copy-start(f32[8,9]{1,0:T(8,128)} %param.11) | copy-start | bytes 868

commit v3 on v2

--- a/solution.py
+++ b/solution.py
@@ -19,13 +19,15 @@
         acc_ref[...] += amp * amp
         return carry
 
-    lax.fori_loop(0, bt_ref.shape[0], body, 0)
+    lax.fori_loop(0, bt_ref.shape[0], body, 0, unroll=4)
     out_ref[...] = acc_ref[...] * dw_ref[...].astype(jnp.float32) * inv_count
 
 
-def coupling_call(bt, pt, dw, inv_count, tile=512):
+def coupling_call(bt, pt, dw, inv_count, tile=2304):
     comps, rows, m = bt.shape
     cols = pt.shape[1]
+    while cols % tile:
+        tile //= 2
     return pl.pallas_call(
         partial(coupling_kernel, inv_count=inv_count),
         grid=(cols // tile,),

time: 254 us -> 214 us (0.84)
  Pallas kernels: 72.1 us -> 32.2 us
    pallas_call x1, Pallas kernels: 72.1 us -> 32.2 us  [coupling_call(): pl.pallas_call(partial(coupling_kernel, inv_count=inv_count), grid=(cols...]
  transfers between devices with their start and end apart: 2 -> 2, of which waited for: 1 -> 1; matrix products, arithmetic and copies ran while one was open for 7% -> 9% of each run, Pallas kernels for 0% -> 0%
where the time goes in v3:
time: 214 us; the launch traced here: 213 us
  local copies, waits for them, and re-layouts  67.3 us (31%)
  blocking collectives  57.6 us (27%)
  Pallas kernels  32.2 us (15%)
  starting transfers between devices  27.9 us (13%)
  other arithmetic  15.9 us (7%)
  waiting for transfers between devices  11.7 us (5%)
    pallas_call x1, Pallas kernels, coupling_call(): pl.pallas_call(partial(coupling_kernel, inv_count=inv_count), grid=(cols...  32.2 us
    all_to_all x2, starting transfers between devices, gather_pb(): got = lax.all_to_all(copies, 'pb', 0, 0, tiled=True)  27.9 us
    gather x4, local copies, waits for them, and re-layouts, on_device(): partner_value = deviation_all[partner]  22.8 us
    psum x3, blocking collectives, branch_total(): summed = lax.psum(partial_sum, 'br')  22.5 us
    all_to_all x1, blocking collectives, on_device(): lax.all_to_all(partials, axes, 0, 0, tiled=True)  18.4 us
    mul x4, local copies, waits for them, and re-layouts, on_device(): spread = jnp.sum(coupling * combined, axis=2)  17.5 us
    all_to_all x1, blocking collectives, gather_pb(): got = lax.all_to_all(copies, 'pb', 0, 0, tiled=True)  16.7 us
    all_to_all x2, waiting for transfers between devices, gather_pb(): got = lax.all_to_all(copies, 'pb', 0, 0, tiled=True)  11.7 us
  transfers between devices with their start and end apart: 2, of which 1 were waited for; matrix products, arithmetic and copies ran while one was open for 9% of the time, Pallas kernels for 0%

profile of v3, /device:TPU:1, one launch (start us, length us, event | category | flops | bytes accessed | tf_op | source)
XLA Modules:
  0.0 213.3 jit_solution(17736019298808744728)
XLA Ops:
  1.5 2.5 %reshape.74 = bf16[64,2,1296]{2,1,0:T(2,128)(2,1)} reshape(bf16[64,9,8,36]{3,2,1,0:T(8,128)(2,1)S(1)} %broadcast_in_dim.10) | data formatting | bytes 663552
  4.0 15.3 %all-to-all-start = ((bf16[64,2,1296]{2,1,0:T(2,128)(2,1)}), bf16[64,2,1296]{2,1,0:T(2,128)(2,1)}, u32[]{:S(2)}, u32[]{:S(2)}) async-start(bf16[64,2,1296]{2,1,0:T(2,128)(2,1)} %reshape.74), calls=%async_computation | async-start | bytes 720896 | tf_op jit(solution)/shard_map/all_to_all | solution.py:54
  19.4 4.3 %reshape.46 = bf16[36,8,36,36]{3,2,1,0:T(8,128)(2,1)S(1)} reshape(bf16[36,10368]{1,0:T(8,128)(2,1)} %param.6) | data formatting | bytes 1492992 | tf_op jit(solution)/shard_map/reshape | solution.py:72
  23.7 2.5 %reshape.73 = bf16[36,288,36]{0,1,2:T(8,128)(2,1)} reshape(bf16[36,8,36,36]{0,2,1,3:T(8,128)(2,1)S(1)} %bitcast.35) | data formatting | bytes 1492992 | tf_op jit(solution)/shard_map/reshape | solution.py:73
  26.2 5.3 %copy.45.bt_ref = bf16[36,288,36]{2,1,0:T(8,128)(2,1)} copy(bf16[36,288,36]{0,1,2:T(8,128)(2,1)} %reshape.73) | data formatting | bytes 1492992 | tf_op jit(solution)/shard_map/reshape | solution.py:73
  31.6 3.5 %copy.43 = bf16[9,512,288]{2,1,0:T(8,128)(2,1)S(1)} copy(bf16[9,512,288]{1,2,0:T(8,128)(2,1)} %param.8) | data formatting | bytes 5308416 | tf_op args[2]
  35.0 2.9 %copy.44 = bf16[4608,288]{0,1:T(8,128)(2,1)} copy(bf16[4608,288]{1,0:T(8,128)(2,1)S(1)} %bitcast.34) | data formatting | bytes 5308416 | tf_op jit(solution)/shard_map/reshape | solution.py:76
  41.8 32.2 %shard_map.77 = f32[288,4608]{1,0:T(8,128)} custom-call(bf16[36,288,36]{2,1,0:T(8,128)(2,1)} %copy.45.bt_ref, bf16[36,4608]{1,0:T(8,128)(2,1)} %copy.53.pt_ref, bf16[288,4608]{1,0:T(8,128)(2,1)} %bitcast.36), custom_call_target="tpu_custom_call" | custom-call | tf_op jit(solution)/shard_map/pallas_call | solution.py:31
  74.0 2.9 %reduce_sum.60 = f32[288]{0:T(512)S(1)} reduce(f32[288,4608]{1,0:T(8,128)} %shard_map.77, f32[]{:T(128)} %constant.8.clone.1), dimensions={1}, to_apply=%region_0.0 | reduce | flops 1326816 | bytes 5309572 | tf_op jit(solution)/shard_map/reduce_sum | solution.py:79
  76.9 6.0 %psum.21 = f32[8,36]{1,0:T(8,128)S(1)} all-reduce(f32[8,36]{1,0:T(8,128)S(1)} %reduce_sum.61), channel_id=1, replica_groups=mesh['pb'=64,'br'=4] {'br'}, use_global_device_ids=true, to_apply=%region_1.0 | all-reduce | flops 288 | bytes 2304 | tf_op jit(solution)/shard_map/psum | solution.py:47
  83.7 12.5 %all-to-all-start.1 = ((f32[64,8,9]{2,1,0:T(8,128)}), f32[64,8,9]{2,1,0:T(8,128)S(1)}, u32[]{:S(2)}, u32[]{:S(2)}) async-start(f32[64,8,9]{2,1,0:T(8,128)} %broadcast_in_dim.11), calls=%async_computation.1 | async-start | bytes 524288 | tf_op jit(solution)/shard_map/all_to_all | solution.py:54
  96.2 11.7 %all-to-all-done.1 = f32[64,8,9]{2,1,0:T(8,128)S(1)} async-done(((f32[64,8,9]{2,1,0:T(8,128)}), f32[64,8,9]{2,1,0:T(8,128)S(1)}, u32[]{:S(2)}, u32[]{:S(2)}) %all-to-all-start.1) | async-done | bytes 18464 | tf_op jit(solution)/shard_map/all_to_all | solution.py:54
  108.0 10.8 %gather_fusion = f32[4096,9]{1,0:T(8,128)S(1)} fusion(f32[512,9]{1,0:T(8,128)S(1)} %bitcast.31, s32[4096]{0:T(1024)S(1)} %broadcast_clamp_fusion), kind=kCustom, calls=%fused_computation | custom fusion | bytes 311296 | tf_op jit(solution)/shard_map/gather | solution.py:85
  119.5 3.2 %mul.51 = f32[8,36,4608]{2,1,0:T(8,128)} broadcast(f32[8,4608]{1,0:T(8,128)S(1)} %bitcast.41), dimensions={0,2} | broadcast | bytes 5455872 | tf_op jit(solution)/shard_map/mul | solution.py:88
  122.7 5.5 %mul.52 = f32[288,4608]{1,0:T(8,128)} reshape(f32[8,36,4608]{2,1,0:T(8,128)} %mul.51) | data formatting | bytes 10616832 | tf_op jit(solution)/shard_map/mul | solution.py:88
  128.2 4.6 %multiply_reduce_fusion.1 = f32[288]{0:T(512)S(1)} fusion(f32[288,4608]{1,0:T(8,128)} %shard_map.77, f32[288,4608]{1,0:T(8,128)} %mul.52), kind=kLoop, calls=%fused_computation.3 | loop fusion | flops 2653920 | bytes 10617984 | tf_op jit(solution)/shard_map/reduce_sum | solution.py:88
  132.9 8.3 %psum.22 = f32[8,36]{1,0:T(8,128)S(1)} all-reduce(f32[8,36]{1,0:T(8,128)S(1)} %reduce_sum.63), channel_id=1, replica_groups=mesh['pb'=64,'br'=4] {'br'}, use_global_device_ids=true, to_apply=%region_3.0 | all-reduce | flops 288 | bytes 2304 | tf_op jit(solution)/shard_map/psum | solution.py:47
  141.3 16.7 %all_to_all.21 = f32[64,8,9]{2,1,0:T(8,128)S(1)} all-to-all(f32[64,8,9]{2,1,0:T(8,128)S(1)} %broadcast_in_dim.13), channel_id=1, replica_groups=mesh['pb'=64,'br'=4] {'pb'}, dimensions={0} | all-to-all | bytes 36864 | tf_op jit(solution)/shard_map/all_to_all | solution.py:54
  158.1 10.8 %gather_fusion.1 = f32[4096,9]{1,0:T(8,128)S(1)} fusion(f32[512,9]{1,0:T(8,128)S(1)} %bitcast.33, s32[4096]{0:T(1024)S(1)} %broadcast_clamp_fusion), kind=kCustom, calls=%fused_computation.1 | custom fusion | bytes 311296 | tf_op jit(solution)/shard_map/gather | solution.py:85
  169.5 3.2 %mul.56 = f32[8,36,4608]{2,1,0:T(8,128)} broadcast(f32[8,4608]{1,0:T(8,128)S(1)} %bitcast.42), dimensions={0,2} | broadcast | bytes 5455872 | tf_op jit(solution)/shard_map/mul | solution.py:88
  172.7 5.5 %mul.57 = f32[288,4608]{1,0:T(8,128)} reshape(f32[8,36,4608]{2,1,0:T(8,128)} %mul.56) | data formatting | bytes 10616832 | tf_op jit(solution)/shard_map/mul | solution.py:88
  178.3 4.7 %multiply_reduce_fusion = f32[288]{0:T(512)S(1)} fusion(f32[288,4608]{1,0:T(8,128)} %shard_map.77, f32[288,4608]{1,0:T(8,128)} %mul.57), kind=kLoop, calls=%fused_computation.2 | loop fusion | flops 2653920 | bytes 10617984 | tf_op jit(solution)/shard_map/reduce_sum | solution.py:88
  183.0 8.3 %psum.23 = f32[8,36]{1,0:T(8,128)S(1)} all-reduce(f32[8,36]{1,0:T(8,128)S(1)} %reduce_sum.65), channel_id=1, replica_groups=mesh['pb'=64,'br'=4] {'br'}, use_global_device_ids=true, to_apply=%region_5.0 | all-reduce | flops 288 | bytes 2304 | tf_op jit(solution)/shard_map/psum | solution.py:47
  194.1 18.4 %all_to_all.22 = f32[256,1,2]{2,1,0:T(1,128)S(1)} all-to-all(f32[256,1,2]{2,1,0:T(1,128)S(1)} %broadcast_in_dim.14), channel_id=1, replica_groups=mesh['pb'=64,'br'=4] {'pb','br'}, dimensions={0} | all-to-all | bytes 4096 | tf_op jit(solution)/shard_map/all_to_all | solution.py:95
  (32 shorter events, 11.0 us)
Async XLA Ops:
  0.6 18.7 %copy-start.1 = (s32[8,512]{1,0:T(8,128)S(1)}, s32[8,512]{1,0:T(8,128)}, u32[]{:S(2)}) copy-start(s32[8,512]{1,0:T(8,128)} %param.9) | copy-start | bytes 49156
  4.0 34.0 %all-to-all-start = ((bf16[64,2,1296]{2,1,0:T(2,128)(2,1)}), bf16[64,2,1296]{2,1,0:T(2,128)(2,1)}, u32[]{:S(2)}, u32[]{:S(2)}) async-start(bf16[64,2,1296]{2,1,0:T(2,128)(2,1)} %reshape.74), calls=%async_computation | async-start | bytes 720896 | tf_op jit(solution)/shard_map/all_to_all | solution.py:54
  74.0 8.9 %copy-start = (f32[8,9]{1,0:T(8,128)S(1)}, f32[8,9]{1,0:T(8,128)}, u32[]{:S(2)}) copy-start(f32[8,9]{1,0:T(8,128)} %param.10) | copy-start | bytes 868
  83.7 24.2 %all-to-all-start.1 = ((f32[64,8,9]{2,1,0:T(8,128)}), f32[64,8,9]{2,1,0:T(8,128)S(1)}, u32[]{:S(2)}, u32[]{:S(2)}) async-start(f32[64,8,9]{2,1,0:T(8,128)} %broadcast_in_dim.11), calls=%async_computation.1 | async-start | bytes 524288 | tf_op jit(solution)/shard_map/all_to_all | solution.py:54
  178.2 13.0 %copy-start.2 = (f32[8,9]{1,0:T(8,128)S(1)}, f32[8,9]{1,0:T(8,128)}, u32[]{:S(2)}) copy-start(f32[8,9]{1,0:T(8,128)} %param.11) | copy-start | bytes 868
